TPU v7x, 256 devices: a whole 4x4x8 slice. The times are simulated.
256 devices in a mesh: wide: 64 (over z, x, core), narrow: 4 (over y).
Axes of the slice: x: 4, y: 4, z: 8, core: 2. Of those that a mesh axis runs over, the one named last changes fastest.
Arguments:
- coeffs: bfloat16 [2, 1024, 1024, 512], P(None, 'wide', None, 'narrow'), may hold values from -3 to 3
- legendre: bfloat16 [1024, 64, 1024], P('wide'), may hold values from -3 to 3
- order_table: int32 [1024], replicated, may hold values from 0 to 1023, each once
- thresholds: float32 [512], replicated, may hold values from 0.2 to 2
Outputs:
- lowrank: float32 [64, 2048, 512], P('wide', 'narrow')
- sparse: float32 [64, 2048, 512], P('wide', 'narrow')
Inputs may be any that keep to these rules, and one draw needn't show every extreme that they name: `order_table`: each order 0 to 1023 stands in exactly one slot.
All inputs are finite; a program needn't handle non-finite values.
Results may differ from a plain program's by a relative error of at most 0.0003.
Values sent between devices are 32-bit elements; how exact they have to be, the bound alone decides.
A program may use at most 128 MiB of HBM per device.

v0:
```python
import math
import jax
import jax.numpy as jnp
from jax import lax
from jax.sharding import PartitionSpec as P

NPIX = 2048
ITERS = 2


def soft_shrink(values, limits):
    return jnp.sign(values) * jnp.maximum(jnp.abs(values) - limits, 0.0)


def wiener_filter(covariance):
    chan_total = covariance.shape[0]
    ridge_shift = jnp.trace(covariance) / chan_total
    factor = jnp.linalg.cholesky(
        covariance + ridge_shift * jnp.eye(chan_total, dtype=covariance.dtype)
    )
    return jax.scipy.linalg.cho_solve((factor, True), covariance)


def per_device(coeffs, legendre, order_table, thresholds):
    slot_count = legendre.shape[0]
    degrees = legendre.shape[2]
    first_slot = lax.axis_index("wide") * slot_count
    own_orders = lax.dynamic_slice_in_dim(order_table, first_slot, slot_count)
    degree_mask = (
        lax.broadcasted_iota(jnp.int32, (slot_count, degrees), 1) >= own_orders[:, None]
    ).astype(legendre.dtype)
    masked = legendre * degree_mask[:, None, :]
    spectra = jnp.einsum("srl,kslc->ksrc", masked, coeffs, preferred_element_type=jnp.float32)
    pixels = lax.broadcasted_iota(jnp.int32, (1, NPIX), 1)
    pixel_phase = order_table[:, None] * pixels % NPIX
    pixel_angle = pixel_phase.astype(jnp.float32) * (2.0 * math.pi / NPIX)
    weights = jnp.where(order_table == 0, 1.0, 2.0).astype(jnp.float32)[:, None]
    cycle_table = jnp.stack([weights * jnp.cos(pixel_angle), -weights * jnp.sin(pixel_angle)])
    sky_map = jnp.einsum(
        "ksrc,ksj->rjc",
        lax.all_to_all(spectra, "wide", split_axis=2, concat_axis=1, tiled=True),
        cycle_table,
        precision=lax.Precision.HIGHEST,
        preferred_element_type=jnp.float32,
    )
    spectra_rows = lax.all_to_all(sky_map, "narrow", split_axis=1, concat_axis=2, tiled=True)
    cycle_count, pixel_count, chan_count = spectra_rows.shape
    sky_field = spectra_rows.reshape(cycle_count * pixel_count, chan_count)
    lowrank = jnp.zeros_like(sky_field)
    sparse = jnp.zeros_like(sky_field)
    for iteration in range(ITERS):
        sparse = soft_shrink(sky_field - lowrank, thresholds)
        residue = sky_field - sparse
        partial_cov = jnp.dot(
            residue.T, residue, precision=lax.Precision.HIGHEST, preferred_element_type=jnp.float32
        )
        covariance = lax.psum(partial_cov, ("wide", "narrow"))
        lowrank = jnp.dot(
            residue,
            wiener_filter(covariance),
            precision=lax.Precision.HIGHEST,
            preferred_element_type=jnp.float32,
        )
    return (
        lowrank.reshape(cycle_count, pixel_count, chan_count),
        sparse.reshape(cycle_count, pixel_count, chan_count),
    )


def solution(mesh):
    placed = (P(None, "wide", None, "narrow"), P("wide", None, None), P(), P())
    return jax.shard_map(
        per_device,
        mesh=mesh,
        in_specs=placed,
        out_specs=(P("wide", "narrow", None), P("wide", "narrow", None)),
        check_vma=False,
    )
```

profile of v0, /device:TPU:2, one launch (start us, length us, event | category | flops | bytes accessed | tf_op | source)
XLA Modules:
  0.0 966.5 jit_solution(3870654779187750146)
XLA Ops:
  8.0 5.5 fusion.14
  15.3 12.0 %all-to-all-start = ((f32[2,16,64,128]{3,0,1,2:T(2,128)}), f32[2,16,64,128]{3,0,1,2:T(2,128)S(1)}, u32[]{:S(2)}, u32[]{:S(2)}) async-start(f32[2,16,64,128]{3,0,1,2:T(2,128)} %copy.24), calls=%async_computation | async-start | bytes 2097152 | tf_op jit(solution)/shard_map/all_to_all | solution.py:41
  27.4 35.0 %cosine_multiply_fusion = (f32[1,1024,2048]{1,2,0:T(8,128)}, f32[1,1024,2048]{1,2,0:T(8,128)}) fusion(s32[1024]{0:T(1024)S(1)} %copy-done.7, f32[1024]{0:T(1024)S(1)} %get-tuple-element.68, f32[1024]{0:T(1024)S(1)} %get-tuple-element.69), kind=kLoop, calls=%fused_computation.17 | loop fusion | flops 33554432 | bytes 16789504 | tf_op jit(solution)/shard_map/mul | solution.py:38
  62.4 16.5 %fusion = f32[2048,128,1]{1,0,2:T(8,128)S(1)} fusion(f32[2,1024,128]{2,1,0:T(8,128)S(1)} %bitcast.179, f32[1,1024,2048]{1,2,0:T(8,128)} %get-tuple-element.67, f32[1,1024,2048]{1,2,0:T(8,128)} %get-tuple-element.66), kind=kOutput, calls=%fused_computation.4 | convolution fusion | flops 6446645248 | bytes 18874368 | tf_op jit(solution)/shard_map/ksrc,ksj->rjc/dot_general | solution.py:39
  79.0 19.9 %all_to_all.30 = f32[1,2048,128]{2,0,1:T(1,128)S(1)} all-to-all(f32[1,2048,128]{2,0,1:T(1,128)S(1)} %bitcast.180), channel_id=1, replica_groups=mesh['wide'=64,'narrow'=4] {'narrow'}, dimensions={1} | all-to-all | bytes 2097152 | tf_op jit(solution)/shard_map/all_to_all | solution.py:46
  99.7 2.8 fusion.143
  104.0 256.8 %all-reduce.4.cloned.1.call-done = f32[512,512]{0,1:T(8,128)} async-done(((f32[512,512]{0,1:T(8,128)}), f32[512,512]{0,1:T(8,128)}) %all-reduce.4.cloned.1.call-update) | async-done | bytes 1048592 | tf_op jit(solution)/shard_map/psum | solution.py:57
  368.8 11.7 %cholesky.286 = f32[128,128]{1,0:T(8,128)S(1)} custom-call(f32[128,128]{1,0:T(8,128)S(1)} %cholesky.426), custom_call_target="Cholesky" | custom-call | tf_op jit(solution)/shard_map/jit(cholesky)/cholesky | solution.py:18
  380.5 9.8 %custom-call.29 = f32[1,128,128]{1,2,0:T(8,128)S(1)} custom-call(f32[1,128,128]{2,1,0:T(8,128)S(1)} %get-tuple-element.65), custom_call_target="InvertDiagBlocksLowerTriangular" | custom-call | tf_op jit(solution)/shard_map/jit(cholesky)/cholesky | solution.py:18
  393.0 11.7 %cholesky.305 = f32[128,128]{1,0:T(8,128)S(1)} custom-call(f32[128,128]{1,0:T(8,128)S(1)} %cholesky.430), custom_call_target="Cholesky" | custom-call | tf_op jit(solution)/shard_map/jit(cholesky)/cholesky | solution.py:18
  404.7 18.5 %custom-call.30 = f32[1,128,128]{1,2,0:T(8,128)S(1)} custom-call(f32[1,128,128]{2,1,0:T(8,128)S(1)} %get-tuple-element.62), custom_call_target="InvertDiagBlocksLowerTriangular" | custom-call | tf_op jit(solution)/shard_map/jit(cholesky)/cholesky | solution.py:18
  424.8 11.7 %cholesky.326 = f32[128,128]{1,0:T(8,128)S(1)} custom-call(f32[128,128]{1,0:T(8,128)S(1)} %cholesky.435), custom_call_target="Cholesky" | custom-call | tf_op jit(solution)/shard_map/jit(cholesky)/cholesky | solution.py:18
  437.2 9.8 %custom-call.31 = f32[1,128,128]{1,2,0:T(8,128)S(1)} custom-call(f32[1,128,128]{2,1,0:T(8,128)S(1)} %get-tuple-element.59), custom_call_target="InvertDiagBlocksLowerTriangular" | custom-call | tf_op jit(solution)/shard_map/jit(cholesky)/cholesky | solution.py:18
  448.5 12.1 %cholesky.343 = f32[128,128]{1,0:T(8,128)S(1)} custom-call(f32[128,128]{1,0:T(8,128)S(1)} %convolution_subtract_fusion.18), custom_call_target="Cholesky" | custom-call | tf_op jit(solution)/shard_map/jit(cholesky)/cholesky | solution.py:18
  465.6 11.2 %while.4 = (s32[]{:T(128)}, f32[512,512]{1,0:T(8,128)}, s32[4,2]{0,1:T(2,128)S(1)}, f32[4,128,128]{2,1,0:T(8,128)S(1)}, s32[]{:T(128)}) while((s32[]{:T(128)}, f32[512,512]{1,0:T(8,128)}, s32[4,2]{0,1:T(2,128)S(1)}, f32[4,128,128]{2,1,0:T(8,128)S(1)}, s32[]{:T(128)}) %tuple.61), condition=%wide.while_cond, body=%wide.while_body.sunk | while | flops 2 | bytes 131181 | solution.py:21
  477.6 40.1 %custom-call.32 = f32[4,128,128]{1,2,0:T(8,128)S(1)} custom-call(f32[4,128,128]{2,1,0:T(8,128)} %copy-done.5), custom_call_target="InvertDiagBlocksLowerTriangular" | custom-call | tf_op jit(solution)/shard_map/jit(_cho_solve)/triangular_solve | solution.py:21
  522.3 2.4 convolution_subtract_fusion.12
  530.9 3.3 bitcast_subtract_fusion
  534.2 2.9 fusion.144
  537.1 2.5 copy.39
  539.6 255.4 %all-reduce.6.cloned.1.call-done = f32[512,512]{0,1:T(8,128)} async-done(((f32[512,512]{0,1:T(8,128)}), f32[512,512]{0,1:T(8,128)}) %all-reduce.6.cloned.1.call-update) | async-done | bytes 1048592 | tf_op jit(solution)/shard_map/psum | solution.py:57
  803.1 11.9 %cholesky.358 = f32[128,128]{1,0:T(8,128)S(1)} custom-call(f32[128,128]{1,0:T(8,128)S(1)} %cholesky.439), custom_call_target="Cholesky" | custom-call | tf_op jit(solution)/shard_map/jit(cholesky)/cholesky | solution.py:18
  815.1 9.8 %custom-call.33 = f32[1,128,128]{1,2,0:T(8,128)S(1)} custom-call(f32[1,128,128]{2,1,0:T(8,128)S(1)} %get-tuple-element.55), custom_call_target="InvertDiagBlocksLowerTriangular" | custom-call | tf_op jit(solution)/shard_map/jit(cholesky)/cholesky | solution.py:18
  827.5 11.7 %cholesky.377 = f32[128,128]{1,0:T(8,128)S(1)} custom-call(f32[128,128]{1,0:T(8,128)S(1)} %cholesky.443), custom_call_target="Cholesky" | custom-call | tf_op jit(solution)/shard_map/jit(cholesky)/cholesky | solution.py:18
  840.6 10.0 %custom-call.34 = f32[1,128,128]{1,2,0:T(8,128)S(1)} custom-call(f32[1,128,128]{2,1,0:T(8,128)S(1)} %get-tuple-element.52), custom_call_target="InvertDiagBlocksLowerTriangular" | custom-call | tf_op jit(solution)/shard_map/jit(cholesky)/cholesky | solution.py:18
  852.1 11.7 %cholesky.398 = f32[128,128]{1,0:T(8,128)S(1)} custom-call(f32[128,128]{1,0:T(8,128)S(1)} %cholesky.448), custom_call_target="Cholesky" | custom-call | tf_op jit(solution)/shard_map/jit(cholesky)/cholesky | solution.py:18
  864.5 9.8 %custom-call.35 = f32[1,128,128]{1,2,0:T(8,128)S(1)} custom-call(f32[1,128,128]{2,1,0:T(8,128)S(1)} %get-tuple-element.49), custom_call_target="InvertDiagBlocksLowerTriangular" | custom-call | tf_op jit(solution)/shard_map/jit(cholesky)/cholesky | solution.py:18
  875.8 11.7 %cholesky.415 = f32[128,128]{1,0:T(8,128)S(1)} custom-call(f32[128,128]{1,0:T(8,128)S(1)} %convolution_subtract_fusion.17), custom_call_target="Cholesky" | custom-call | tf_op jit(solution)/shard_map/jit(cholesky)/cholesky | solution.py:18
  891.8 11.7 %while.5 = (s32[]{:T(128)}, f32[512,512]{1,0:T(8,128)}, s32[4,2]{0,1:T(2,128)S(1)}, f32[4,128,128]{2,1,0:T(8,128)S(1)}, s32[]{:T(128)}) while((s32[]{:T(128)}, f32[512,512]{1,0:T(8,128)}, s32[4,2]{0,1:T(2,128)S(1)}, f32[4,128,128]{2,1,0:T(8,128)S(1)}, s32[]{:T(128)}) %tuple.71), condition=%wide.while_cond.clone, body=%wide.while_body.clone.sunk | while | flops 2 | bytes 131181 | solution.py:21
  903.6 39.6 %custom-call.36 = f32[4,128,128]{1,2,0:T(8,128)S(1)} custom-call(f32[4,128,128]{2,1,0:T(8,128)S(1)} %get-tuple-element.19), custom_call_target="InvertDiagBlocksLowerTriangular" | custom-call | tf_op jit(solution)/shard_map/jit(_cho_solve)/triangular_solve | solution.py:21
  947.8 2.4 convolution_subtract_fusion.10
  956.3 2.8 convolution_bitcast_fusion
  (128 shorter events, 83.0 us)
Async XLA Ops:
  8.0 19.3 %copy-start.7 = (s32[1024]{0:T(1024)S(1)}, s32[1024]{0:T(1024)}, u32[]{:S(2)}) copy-start(s32[1024]{0:T(1024)} %param.9) | copy-start | bytes 12292
  15.3 47.1 %all-to-all-start = ((f32[2,16,64,128]{3,0,1,2:T(2,128)}), f32[2,16,64,128]{3,0,1,2:T(2,128)S(1)}, u32[]{:S(2)}, u32[]{:S(2)}) async-start(f32[2,16,64,128]{3,0,1,2:T(2,128)} %copy.24), calls=%async_computation | async-start | bytes 2097152 | tf_op jit(solution)/shard_map/all_to_all | solution.py:41
  27.3 333.4 %all-reduce.4.cloned.1.call-start = ((), (), s32[]{:S(2)}) async-start(), calls=%async_computation.2 | async-start | bytes 2097152 | tf_op jit(solution)/shard_map/psum | solution.py:57
  62.4 36.8 %copy-start.6 = (f32[512]{0:T(512)S(1)}, f32[512]{0:T(512)}, u32[]{:S(2)}) copy-start(f32[512]{0:T(512)} %param.10) | copy-start | bytes 6148
  102.5 692.5 %all-reduce.6.cloned.1.call-start = ((), (), s32[]{:S(2)}) async-start(), calls=%async_computation.3 | async-start | bytes 2097152 | tf_op jit(solution)/shard_map/psum | solution.py:57
  360.7 157.0 %copy-start = (f32[512,512]{0,1:T(8,128)S(1)}, f32[512,512]{0,1:T(8,128)}, u32[]{:S(2)}) copy-start(f32[512,512]{0,1:T(8,128)} %all-reduce.4.cloned.1.call-done) | copy-start | bytes 3145732
  367.8 1.0 copy-start.4
  465.6 65.4 %copy-start.2 = (f32[512,512]{0,1:T(8,128)S(1)}, f32[512,512]{0,1:T(8,128)}, u32[]{:S(2)}) copy-start(f32[512,512]{0,1:T(8,128)} %bitcast_subtract_fusion.1) | copy-start | bytes 3145732
  476.8 0.7 copy-start.5
  795.1 148.1 %copy-start.1 = (f32[512,512]{0,1:T(8,128)S(1)}, f32[512,512]{0,1:T(8,128)}, u32[]{:S(2)}) copy-start(f32[512,512]{0,1:T(8,128)} %all-reduce.6.cloned.1.call-done) | copy-start | bytes 3145732
  802.1 1.0 copy-start.3
Sparse Core Ops, SparseCore 0:
  102.6 258.0 all-reduce.3
  537.2 257.7 all-reduce.5
where the time goes:
time: 975 us; the launch traced here: 966 us
  waiting for transfers between devices  512 us (53%)
  other arithmetic  296 us (30%)
  matrix products  71 us (7%)
  local copies, waits for them, and re-layouts  33.9 us (3%)
  between operations  21.4 us (2%)
  blocking collectives  19.9 us (2%)
  starting transfers between devices  12.1 us (1%)
    psum x2, waiting for transfers between devices, per_device(): covariance = lax.psum(partial_cov, ('wide', 'narrow'))  512 us
    another operation x29, other arithmetic, wiener_filter(): jnp.linalg.cholesky(covariance + ridge_shift * jnp.eye(chan_total, dtype=...  167 us
    another operation x5, other arithmetic, wiener_filter(): return jax.scipy.linalg.cho_solve((factor, True), covariance)  81.9 us
    mul x1, other arithmetic, per_device(): weights * jnp.cos(pixel_angle)  35 us
    another operation x28, matrix products, wiener_filter(): return jax.scipy.linalg.cho_solve((factor, True), covariance)  26.2 us
    another operation x27, local copies, waits for them, and re-layouts, wiener_filter(): return jax.scipy.linalg.cho_solve((factor, True), covariance)  22.8 us
    all_to_all x1, blocking collectives, per_device(): lax.all_to_all(sky_map, 'narrow', split_axis=1, concat_axis=2, tiled=True)  19.9 us
  transfers between devices with their start and end apart: 3, of which 2 were waited for; matrix products, arithmetic and copies ran while one was open for 4% of the time, Pallas kernels for 0%

commit v1 on v0

--- a/solution.py
+++ b/solution.py
@@ -54,7 +54,7 @@
         partial_cov = jnp.dot(
             residue.T, residue, precision=lax.Precision.HIGHEST, preferred_element_type=jnp.float32
         )
-        covariance = lax.psum(partial_cov, ("wide", "narrow"))
+        covariance = lax.psum(lax.psum(partial_cov, "narrow"), "wide")
         lowrank = jnp.dot(
             residue,
             wiener_filter(covariance),

time: 975 us -> 941 us (0.965)
  waiting for transfers between devices: 512 us -> 477 us
    psum x2 -> x4, waiting for transfers between devices: 512 us -> 477 us  [per_device(): covariance = lax.psum(lax.psum(partial_cov, 'narrow'), 'wide')]
  transfers between devices with their start and end apart: 3 -> 5, of which waited for: 2 -> 4; matrix products, arithmetic and copies ran while one was open for 4% -> 4% of each run, Pallas kernels for 0% -> 0%
where the time goes in v1:
time: 941 us; the launch traced here: 932 us
  waiting for transfers between devices  477 us (51%)
  other arithmetic  296 us (31%)
  matrix products  70.9 us (8%)
  local copies, waits for them, and re-layouts  34.3 us (4%)
  between operations  21.2 us (2%)
  blocking collectives  19.9 us (2%)
  starting transfers between devices  12.3 us (1%)
    psum x4, waiting for transfers between devices, per_device(): covariance = lax.psum(lax.psum(partial_cov, 'narrow'), 'wide')  477 us
    another operation x29, other arithmetic, wiener_filter(): jnp.linalg.cholesky(covariance + ridge_shift * jnp.eye(chan_total, dtype=...  167 us
    another operation x5, other arithmetic, wiener_filter(): return jax.scipy.linalg.cho_solve((factor, True), covariance)  81.6 us
    mul x1, other arithmetic, per_device(): weights * jnp.cos(pixel_angle)  35 us
    another operation x28, matrix products, wiener_filter(): return jax.scipy.linalg.cho_solve((factor, True), covariance)  26.2 us
    another operation x27, local copies, waits for them, and re-layouts, wiener_filter(): return jax.scipy.linalg.cho_solve((factor, True), covariance)  23.3 us
    all_to_all x1, blocking collectives, per_device(): lax.all_to_all(sky_map, 'narrow', split_axis=1, concat_axis=2, tiled=True)  19.9 us
  transfers between devices with their start and end apart: 5, of which 4 were waited for; matrix products, arithmetic and copies ran while one was open for 4% of the time, Pallas kernels for 0%

profile of v1, /device:TPU:2, one launch (start us, length us, event | category | flops | bytes accessed | tf_op | source)
XLA Modules:
  0.0 931.9 jit_solution(15211154648451930842)
XLA Ops:
  8.0 5.5 fusion.14
  15.3 12.0 %all-to-all-start = ((f32[2,16,64,128]{3,0,1,2:T(2,128)}), f32[2,16,64,128]{3,0,1,2:T(2,128)S(1)}, u32[]{:S(2)}, u32[]{:S(2)}) async-start(f32[2,16,64,128]{3,0,1,2:T(2,128)} %copy.24), calls=%async_computation | async-start | bytes 2097152 | tf_op jit(solution)/shard_map/all_to_all | solution.py:41
  27.4 35.0 %cosine_multiply_fusion = (f32[1,1024,2048]{1,2,0:T(8,128)}, f32[1,1024,2048]{1,2,0:T(8,128)}) fusion(s32[1024]{0:T(1024)S(1)} %copy-done.7, f32[1024]{0:T(1024)S(1)} %get-tuple-element.68, f32[1024]{0:T(1024)S(1)} %get-tuple-element.69), kind=kLoop, calls=%fused_computation.17 | loop fusion | flops 33554432 | bytes 16789504 | tf_op jit(solution)/shard_map/mul | solution.py:38
  62.4 16.5 %fusion = f32[2048,128,1]{1,0,2:T(8,128)S(1)} fusion(f32[2,1024,128]{2,1,0:T(8,128)S(1)} %bitcast.179, f32[1,1024,2048]{1,2,0:T(8,128)} %get-tuple-element.67, f32[1,1024,2048]{1,2,0:T(8,128)} %get-tuple-element.66), kind=kOutput, calls=%fused_computation.4 | convolution fusion | flops 6446645248 | bytes 18874368 | tf_op jit(solution)/shard_map/ksrc,ksj->rjc/dot_general | solution.py:39
  79.0 19.9 %all_to_all.30 = f32[1,2048,128]{2,0,1:T(1,128)S(1)} all-to-all(f32[1,2048,128]{2,0,1:T(1,128)S(1)} %bitcast.180), channel_id=1, replica_groups=mesh['wide'=64,'narrow'=4] {'narrow'}, dimensions={1} | all-to-all | bytes 2097152 | tf_op jit(solution)/shard_map/all_to_all | solution.py:46
  99.7 2.8 fusion.143
  102.6 50.6 %all-reduce.6.cloned.1.call-done = f32[512,512]{0,1:T(8,128)} async-done(((f32[512,512]{0,1:T(8,128)}), f32[512,512]{0,1:T(8,128)}) %all-reduce.6.cloned.1.call-update) | async-done | bytes 1048592 | tf_op jit(solution)/shard_map/psum | solution.py:57
  154.6 189.8 %all-reduce.8.cloned.1.call-done = f32[512,512]{0,1:T(8,128)} async-done(((f32[512,512]{0,1:T(8,128)}), f32[512,512]{0,1:T(8,128)}) %all-reduce.8.cloned.1.call-update) | async-done | bytes 1048592 | tf_op jit(solution)/shard_map/psum | solution.py:57
  352.5 11.7 %cholesky.286 = f32[128,128]{1,0:T(8,128)S(1)} custom-call(f32[128,128]{1,0:T(8,128)S(1)} %cholesky.426), custom_call_target="Cholesky" | custom-call | tf_op jit(solution)/shard_map/jit(cholesky)/cholesky | solution.py:18
  364.2 9.8 %custom-call.29 = f32[1,128,128]{1,2,0:T(8,128)S(1)} custom-call(f32[1,128,128]{2,1,0:T(8,128)S(1)} %get-tuple-element.65), custom_call_target="InvertDiagBlocksLowerTriangular" | custom-call | tf_op jit(solution)/shard_map/jit(cholesky)/cholesky | solution.py:18
  376.7 11.7 %cholesky.305 = f32[128,128]{1,0:T(8,128)S(1)} custom-call(f32[128,128]{1,0:T(8,128)S(1)} %cholesky.430), custom_call_target="Cholesky" | custom-call | tf_op jit(solution)/shard_map/jit(cholesky)/cholesky | solution.py:18
  388.4 18.5 %custom-call.30 = f32[1,128,128]{1,2,0:T(8,128)S(1)} custom-call(f32[1,128,128]{2,1,0:T(8,128)S(1)} %get-tuple-element.62), custom_call_target="InvertDiagBlocksLowerTriangular" | custom-call | tf_op jit(solution)/shard_map/jit(cholesky)/cholesky | solution.py:18
  408.5 11.7 %cholesky.326 = f32[128,128]{1,0:T(8,128)S(1)} custom-call(f32[128,128]{1,0:T(8,128)S(1)} %cholesky.435), custom_call_target="Cholesky" | custom-call | tf_op jit(solution)/shard_map/jit(cholesky)/cholesky | solution.py:18
  421.0 9.8 %custom-call.31 = f32[1,128,128]{1,2,0:T(8,128)S(1)} custom-call(f32[1,128,128]{2,1,0:T(8,128)S(1)} %get-tuple-element.59), custom_call_target="InvertDiagBlocksLowerTriangular" | custom-call | tf_op jit(solution)/shard_map/jit(cholesky)/cholesky | solution.py:18
  432.3 12.1 %cholesky.343 = f32[128,128]{1,0:T(8,128)S(1)} custom-call(f32[128,128]{1,0:T(8,128)S(1)} %convolution_subtract_fusion.18), custom_call_target="Cholesky" | custom-call | tf_op jit(solution)/shard_map/jit(cholesky)/cholesky | solution.py:18
  449.4 11.7 %while.4 = (s32[]{:T(128)}, f32[512,512]{1,0:T(8,128)}, s32[4,2]{0,1:T(2,128)S(1)}, f32[4,128,128]{2,1,0:T(8,128)S(1)}, s32[]{:T(128)}) while((s32[]{:T(128)}, f32[512,512]{1,0:T(8,128)}, s32[4,2]{0,1:T(2,128)S(1)}, f32[4,128,128]{2,1,0:T(8,128)S(1)}, s32[]{:T(128)}) %tuple.61), condition=%wide.while_cond, body=%wide.while_body.sunk | while | flops 2 | bytes 131181 | solution.py:21
  461.8 40.1 %custom-call.32 = f32[4,128,128]{1,2,0:T(8,128)S(1)} custom-call(f32[4,128,128]{2,1,0:T(8,128)} %copy-done.5), custom_call_target="InvertDiagBlocksLowerTriangular" | custom-call | tf_op jit(solution)/shard_map/jit(_cho_solve)/triangular_solve | solution.py:21
  515.1 3.3 bitcast_subtract_fusion
  518.4 2.8 fusion.144
  521.5 48.4 %all-reduce.10.cloned.1.call-done = f32[512,512]{0,1:T(8,128)} async-done(((f32[512,512]{0,1:T(8,128)}), f32[512,512]{0,1:T(8,128)}) %all-reduce.10.cloned.1.call-update) | async-done | bytes 1048592 | tf_op jit(solution)/shard_map/psum | solution.py:57
  569.9 2.5 copy.39
  572.4 188.6 %all-reduce.12.cloned.1.call-done = f32[512,512]{0,1:T(8,128)} async-done(((f32[512,512]{0,1:T(8,128)}), f32[512,512]{0,1:T(8,128)}) %all-reduce.12.cloned.1.call-update) | async-done | bytes 1048592 | tf_op jit(solution)/shard_map/psum | solution.py:57
  769.0 11.7 %cholesky.358 = f32[128,128]{1,0:T(8,128)S(1)} custom-call(f32[128,128]{1,0:T(8,128)S(1)} %cholesky.439), custom_call_target="Cholesky" | custom-call | tf_op jit(solution)/shard_map/jit(cholesky)/cholesky | solution.py:18
  780.9 9.8 %custom-call.33 = f32[1,128,128]{1,2,0:T(8,128)S(1)} custom-call(f32[1,128,128]{2,1,0:T(8,128)S(1)} %get-tuple-element.55), custom_call_target="InvertDiagBlocksLowerTriangular" | custom-call | tf_op jit(solution)/shard_map/jit(cholesky)/cholesky | solution.py:18
  793.2 11.7 %cholesky.377 = f32[128,128]{1,0:T(8,128)S(1)} custom-call(f32[128,128]{1,0:T(8,128)S(1)} %cholesky.443), custom_call_target="Cholesky" | custom-call | tf_op jit(solution)/shard_map/jit(cholesky)/cholesky | solution.py:18
  806.3 10.0 %custom-call.34 = f32[1,128,128]{1,2,0:T(8,128)S(1)} custom-call(f32[1,128,128]{2,1,0:T(8,128)S(1)} %get-tuple-element.52), custom_call_target="InvertDiagBlocksLowerTriangular" | custom-call | tf_op jit(solution)/shard_map/jit(cholesky)/cholesky | solution.py:18
  817.9 11.7 %cholesky.398 = f32[128,128]{1,0:T(8,128)S(1)} custom-call(f32[128,128]{1,0:T(8,128)S(1)} %cholesky.448), custom_call_target="Cholesky" | custom-call | tf_op jit(solution)/shard_map/jit(cholesky)/cholesky | solution.py:18
  830.3 9.8 %custom-call.35 = f32[1,128,128]{1,2,0:T(8,128)S(1)} custom-call(f32[1,128,128]{2,1,0:T(8,128)S(1)} %get-tuple-element.49), custom_call_target="InvertDiagBlocksLowerTriangular" | custom-call | tf_op jit(solution)/shard_map/jit(cholesky)/cholesky | solution.py:18
  841.6 11.9 %cholesky.415 = f32[128,128]{1,0:T(8,128)S(1)} custom-call(f32[128,128]{1,0:T(8,128)S(1)} %convolution_subtract_fusion.17), custom_call_target="Cholesky" | custom-call | tf_op jit(solution)/shard_map/jit(cholesky)/cholesky | solution.py:18
  857.9 11.7 %while.5 = (s32[]{:T(128)}, f32[512,512]{1,0:T(8,128)}, s32[4,2]{0,1:T(2,128)S(1)}, f32[4,128,128]{2,1,0:T(8,128)S(1)}, s32[]{:T(128)}) while((s32[]{:T(128)}, f32[512,512]{1,0:T(8,128)}, s32[4,2]{0,1:T(2,128)S(1)}, f32[4,128,128]{2,1,0:T(8,128)S(1)}, s32[]{:T(128)}) %tuple.75), condition=%wide.while_cond.clone, body=%wide.while_body.clone.sunk | while | flops 2 | bytes 131181 | solution.py:21
  869.6 39.3 %custom-call.36 = f32[4,128,128]{1,2,0:T(8,128)S(1)} custom-call(f32[4,128,128]{2,1,0:T(8,128)S(1)} %get-tuple-element.19), custom_call_target="InvertDiagBlocksLowerTriangular" | custom-call | tf_op jit(solution)/shard_map/jit(_cho_solve)/triangular_solve | solution.py:21
  922.1 2.8 convolution_bitcast_fusion
  (134 shorter events, 88.6 us)
Async XLA Ops:
  8.0 19.3 %copy-start.7 = (s32[1024]{0:T(1024)S(1)}, s32[1024]{0:T(1024)}, u32[]{:S(2)}) copy-start(s32[1024]{0:T(1024)} %param.9) | copy-start | bytes 12292
  15.3 47.1 %all-to-all-start = ((f32[2,16,64,128]{3,0,1,2:T(2,128)}), f32[2,16,64,128]{3,0,1,2:T(2,128)S(1)}, u32[]{:S(2)}, u32[]{:S(2)}) async-start(f32[2,16,64,128]{3,0,1,2:T(2,128)} %copy.24), calls=%async_computation | async-start | bytes 2097152 | tf_op jit(solution)/shard_map/all_to_all | solution.py:41
  27.3 125.9 %all-reduce.6.cloned.1.call-start = ((), (), s32[]{:S(2)}) async-start(), calls=%async_computation.2 | async-start | bytes 2097152 | tf_op jit(solution)/shard_map/psum | solution.py:57
  62.4 36.8 %copy-start.6 = (f32[512]{0:T(512)S(1)}, f32[512]{0:T(512)}, u32[]{:S(2)}) copy-start(f32[512]{0:T(512)} %param.10) | copy-start | bytes 6148
  102.5 241.9 %all-reduce.8.cloned.1.call-start = ((), (), s32[]{:S(2)}) async-start(), calls=%async_computation.3 | async-start | bytes 2097152 | tf_op jit(solution)/shard_map/psum | solution.py:57
  153.2 416.7 %all-reduce.10.cloned.1.call-start = ((), (), s32[]{:S(2)}) async-start(), calls=%async_computation.4 | async-start | bytes 2097152 | tf_op jit(solution)/shard_map/psum | solution.py:57
  344.4 157.5 %copy-start = (f32[512,512]{0,1:T(8,128)S(1)}, f32[512,512]{0,1:T(8,128)}, u32[]{:S(2)}) copy-start(f32[512,512]{0,1:T(8,128)} %all-reduce.8.cloned.1.call-done) | copy-start | bytes 3145732
  351.5 1.0 copy-start.4
  449.3 65.8 %copy-start.2 = (f32[512,512]{0,1:T(8,128)S(1)}, f32[512,512]{0,1:T(8,128)}, u32[]{:S(2)}) copy-start(f32[512,512]{0,1:T(8,128)} %bitcast_subtract_fusion.1) | copy-start | bytes 3145732
  461.1 0.7 copy-start.5
  521.3 239.7 %all-reduce.12.cloned.1.call-start = ((), (), s32[]{:S(2)}) async-start(), calls=%async_computation.5 | async-start | bytes 2097152 | tf_op jit(solution)/shard_map/psum | solution.py:57
  761.0 147.9 %copy-start.1 = (f32[512,512]{0,1:T(8,128)S(1)}, f32[512,512]{0,1:T(8,128)}, u32[]{:S(2)}) copy-start(f32[512,512]{0,1:T(8,128)} %all-reduce.12.cloned.1.call-done) | copy-start | bytes 3145732
  768.0 1.0 copy-start.3
Sparse Core Ops, SparseCore 0:
  102.6 50.4 all-reduce.5
  156.6 187.8 all-reduce.7
  521.4 48.4 all-reduce.9
  573.1 187.7 all-reduce.11
